TPU v7x, 256 devices: a whole 4x4x8 slice. The times are simulated.
256 devices in a mesh: term: 4 (over x), sector: 64 (over y, z, core).
Axes of the slice: x: 4, y: 4, z: 8, core: 2. Of those that a mesh axis runs over, the one named last changes fastest.
Arguments:
- psi_blocks: bfloat16 [4096, 128, 128], P('sector'), may hold values from -6 to 6
- right_ops: bfloat16 [8, 4096, 128, 128], P('term', 'sector'), may hold values from -0.5 to 0.5
- left_ops: bfloat16 [8, 4096, 128, 128], P('term', 'sector'), may hold values from -0.1875 to 0.1875
- owner_map: int32 [4096, 1], P('sector'), may hold values from 0 to 63; in each aligned block of 64 rows (0 to 63, 64 to 127, ...) at most 2 rows name the same one
- left_local: int32 [4096, 1], P('sector'), may hold values from 0 to 63
Outputs:
- sigma: bfloat16 [4096, 128, 128], P('sector', 'term')
Inputs may be any that keep to these rules, and one draw needn't show every extreme that they name: `owner_map`: among the 64 sectors held by one device along `sector` (aligned blocks), at most 2 name the same owner; some block reaches it.
All inputs are finite; a program needn't handle non-finite values.
Results may differ from a plain program's by a relative error of at most 0.0049.
Values may be sent and summed in bfloat16 or wider, within the bound.
A program may use at most 128 MiB of HBM per device.

v0:
```python
import jax
import jax.numpy as jnp
from jax import lax
from jax.sharding import PartitionSpec as P


def ranks_of(owners):
    count = owners.shape[-1]
    same = owners[..., :, None] == owners[..., None, :]
    earlier = lax.broadcasted_iota(jnp.int32, (count, count), 0) < lax.broadcasted_iota(
        jnp.int32, (count, count), 1
    )
    return jnp.sum((same & earlier).astype(jnp.int32), axis=-2)


def local(psi_blocks, right_ops, left_ops, owner_map, left_local):
    sec_dev = psi_blocks.shape[0]
    width = psi_blocks.shape[1]
    terms_dev = right_ops.shape[0]
    n_sector = lax.axis_size("sector")
    capacity = max(2, 2 * sec_dev // n_sector)
    slots = n_sector * capacity
    owners = owner_map[:, 0]
    slot_id = owners * capacity + ranks_of(owners)
    packer = (lax.broadcasted_iota(jnp.int32, (slots, sec_dev), 0) == slot_id[None, :]).astype(
        jnp.bfloat16
    )
    routes_all = lax.all_gather(
        jnp.concatenate([owner_map, left_local], axis=1), "sector", axis=0, tiled=True
    )
    all_owners = routes_all[:, 0].reshape(n_sector, sec_dev)
    all_local = routes_all[:, 1].reshape(n_sector, sec_dev)
    all_ranks = ranks_of(all_owners)
    mine = lax.axis_index("sector")
    slot_iota = lax.broadcasted_iota(jnp.int32, (1, 1, capacity), 2)
    hits = (all_owners == mine)[:, :, None] & (all_ranks[:, :, None] == slot_iota)
    tags = (jnp.sum(jnp.where(hits, all_local[:, :, None] + 1, 0), axis=1) - 1).reshape(slots)
    inter = jnp.einsum(
        "sij,tsjk->stik", psi_blocks, right_ops, preferred_element_type=jnp.float32
    ).astype(jnp.bfloat16)
    packed = jnp.dot(packer, inter.reshape(sec_dev, -1), preferred_element_type=jnp.float32).astype(
        jnp.bfloat16
    )
    arrived = lax.all_to_all(
        packed.reshape(n_sector, capacity, -1), "sector", split_axis=0, concat_axis=0, tiled=True
    )
    arrived = arrived.reshape(slots, terms_dev, width, width)
    picked = jnp.take(left_ops, jnp.clip(tags, 0, sec_dev - 1), axis=1)
    images = jnp.einsum("tnij,ntjk->nik", picked, arrived, preferred_element_type=jnp.float32)
    collect = (lax.broadcasted_iota(jnp.int32, (sec_dev, slots), 0) == tags[None, :]).astype(
        jnp.float32
    )
    partial_sum = jnp.dot(
        collect,
        images.reshape(slots, -1),
        precision=lax.Precision.HIGHEST,
        preferred_element_type=jnp.float32,
    ).reshape(sec_dev, width, width)
    total = lax.psum(partial_sum, "term")
    row_count = width // lax.axis_size("term")
    mine_rows = lax.dynamic_slice_in_dim(total, lax.axis_index("term") * row_count, row_count, 1)
    return mine_rows.astype(jnp.bfloat16)


def solution(mesh):
    placed = (
        P("sector", None, None),
        P("term", "sector", None, None),
        P("term", "sector", None, None),
        P("sector", None),
        P("sector", None),
    )
    return jax.shard_map(
        local, mesh=mesh, in_specs=placed, out_specs=P("sector", "term", None), check_vma=False
    )
```

profile of v0, /device:TPU:1, one launch (start us, length us, event | category | flops | bytes accessed | tf_op | source)
XLA Modules:
  0.0 411.3 jit_solution(9655905848802338681)
XLA Ops:
  0.0 0.0 copy-start
  0.0 0.9 convert_reduce_fusion.1
  0.9 0.7 multiply_add_fusion
  1.6 0.0 copy-done
  1.6 5.4 %convert_bitcast_fusion = bf16[64,2,128,128]{2,3,1,0:T(8,128)(2,1)} fusion(bf16[2,64,128,128]{3,2,1,0:T(8,128)(2,1)} %param.6, bf16[64,128,128]{2,1,0:T(8,128)(2,1)S(1)} %copy-done), kind=kOutput, calls=%fused_computation.12 | convolution fusion | flops 538968064 | bytes 10485760 | tf_op jit(solution)/shard_map/sij,tsjk->stik/dot_general | solution.py:38
  7.0 6.3 %copy.23 = bf16[64,2,128,128]{3,2,1,0:T(8,128)(2,1)} copy(bf16[64,2,128,128]{2,3,1,0:T(8,128)(2,1)} %convert_bitcast_fusion) | data formatting | bytes 8388608 | tf_op jit(solution)/shard_map/convert_element_type | solution.py:40
  13.4 8.8 %convolution_convert_fusion = bf16[128,32768]{1,0:T(8,128)(2,1)} fusion(bf16[8,8,256,128]{3,2,1,0:T(8,128)(2,1)} %bitcast.41, s32[64]{0:T(128)S(1)} %multiply_add_fusion), kind=kOutput, calls=%fused_computation.1 | convolution fusion | flops 541073408 | bytes 12583168 | tf_op jit(solution)/shard_map/dot_general | solution.py:41
  22.1 14.1 %reshape.90 = bf16[64,2,32768]{2,1,0:T(2,128)(2,1)} reshape(bf16[128,32768]{1,0:T(8,128)(2,1)} %convolution_convert_fusion) | data formatting | bytes 16777216 | tf_op jit(solution)/shard_map/reshape | solution.py:45
  36.3 0.0 copy-start.2
  36.3 0.0 copy-start.3
  36.3 13.5 %all-to-all-start = ((bf16[64,2,32768]{2,1,0:T(2,128)(2,1)}), bf16[64,2,32768]{2,1,0:T(2,128)(2,1)}, u32[]{:S(2)}, u32[]{:S(2)}) async-start(bf16[64,2,32768]{2,1,0:T(2,128)(2,1)} %reshape.90), calls=%async_computation | async-start | bytes 16777216 | tf_op jit(solution)/shard_map/all_to_all | solution.py:44
  49.8 0.0 copy-done.2
  49.8 0.0 copy-done.3
  49.8 218.2 %all-gather = s32[64,64,2]{1,2,0:T(2,128)S(1)} all-gather(s32[1,64,2]{1,2,0:T(2,128)S(1)} %add_bitcast_fusion), channel_id=1, replica_groups=mesh['term'=4,'sector'=64] {'sector'}, dimensions={0}, use_global_device_ids=true | all-gather | bytes 33280 | tf_op jit(solution)/shard_map/all_gather | solution.py:28
  268.0 0.1 reshape.102
  268.1 0.1 slice_reduce_fusion
  268.2 0.1 reshape_squeeze.3
  268.3 0.1 add.66
  268.4 0.9 convert_reduce_fusion
  269.3 0.1 select_reduce_fusion
  269.4 0.1 copy.20
  269.5 0.1 sub.7
  269.7 0.1 copy.21
  269.8 0.1 min.18
  269.9 8.6 %gather_fusion = bf16[128,2,128,128]{3,2,1,0:T(8,128)(2,1)} fusion(bf16[2,64,128,128]{3,2,1,0:T(8,128)(2,1)} %param.7, s32[1024]{0:T(1024)S(1)} %pad_clamp_fusion), kind=kCustom, calls=%fused_computation | custom fusion | bytes 16777728 | tf_op jit(solution)/shard_map/jit(_take)/gather | solution.py:48
  278.5 0.0 all-to-all-done
  278.5 14.6 %reshape.91 = bf16[128,2,128,128]{3,2,1,0:T(8,128)(2,1)} reshape(bf16[64,2,32768]{2,1,0:T(2,128)(2,1)} %all-to-all-done) | data formatting | bytes 16777216 | tf_op jit(solution)/shard_map/reshape | solution.py:47
  293.1 8.2 %fusion = f32[128,128,128,1]{2,1,3,0:T(8,128)S(1)} fusion(bf16[128,2,128,128]{3,2,1,0:T(8,128)(2,1)} %reshape.91, bf16[128,2,128,128]{3,2,1,0:T(8,128)(2,1)} %gather_fusion, pred[128]{0:T(512)(128)(4,1)S(1)} %compare_and_fusion), kind=kOutput, calls=%fused_computation.3 | convolution fusion | flops 1077936128 | bytes 25165952 | tf_op jit(solution)/shard_map/tnij,ntjk->nik/dot_general | solution.py:49
  301.3 9.7 %copy.41 = f32[16,8,128,128]{3,1,2,0:T(8,128)} copy(f32[16,8,128,128]{3,2,1,0:T(8,128)S(1)} %bitcast.38) | data formatting | bytes 16777216
  311.1 9.0 %copy.24 = f32[16384,128]{1,0:T(8,128)} copy(f32[16384,128]{0,1:T(8,128)} %bitcast.40) | data formatting | bytes 16777216 | tf_op jit(solution)/shard_map/dot_general | solution.py:53
  320.1 0.0 copy-start.1
  320.1 10.5 %fusion.15 = f32[64,128,128]{2,0,1:T(8,128)} fusion(f32[128,128,128]{2,1,0:T(8,128)} %bitcast.39, s32[128]{0:T(128)S(1)} %sub.7), kind=kOutput, calls=%fused_computation.25 | convolution fusion | flops 1610620928 | bytes 12583424 | tf_op jit(solution)/shard_map/dot_general | solution.py:53
  330.6 78.5 %all-reduce.1 = bf16[64,128,128]{2,0,1:T(8,128)(2,1)} all-reduce(f32[64,128,128]{2,0,1:T(8,128)} %fusion.15), channel_id=1, replica_groups=mesh['term'=4,'sector'=64] {'term'}, use_global_device_ids=true, to_apply=%region_3.4 | all-reduce | flops 1048576 | bytes 6291456 | tf_op jit(solution)/shard_map/psum | solution.py:59
  409.1 1.1 dynamic-slice_convert_fusion
  410.2 1.1 copy.25
  411.3 0.0 copy-done.1
  (8 shorter events, 0.1 us)
Async XLA Ops:
  0.0 1.6 copy-start
  36.3 13.5 %copy-start.2 = (s32[64,1]{0,1:T(1,128)S(1)}, s32[64,1]{0,1:T(1,128)}, u32[]{:S(2)}) copy-start(s32[64,1]{0,1:T(1,128)} %param.8) | copy-start | bytes 772
  36.3 13.5 %copy-start.3 = (s32[64,1]{0,1:T(1,128)S(1)}, s32[64,1]{0,1:T(1,128)}, u32[]{:S(2)}) copy-start(s32[64,1]{0,1:T(1,128)} %param.9) | copy-start | bytes 772
  36.3 242.2 %all-to-all-start = ((bf16[64,2,32768]{2,1,0:T(2,128)(2,1)}), bf16[64,2,32768]{2,1,0:T(2,128)(2,1)}, u32[]{:S(2)}, u32[]{:S(2)}) async-start(bf16[64,2,32768]{2,1,0:T(2,128)(2,1)} %reshape.90), calls=%async_computation | async-start | bytes 16777216 | tf_op jit(solution)/shard_map/all_to_all | solution.py:44
  320.1 91.2 %copy-start.1 = (bf16[64,128,128]{2,1,0:T(8,128)(2,1)S(1)}, bf16[64,128,128]{2,1,0:T(8,128)(2,1)}, u32[]{:S(2)}) copy-start(bf16[64,128,128]{2,1,0:T(8,128)(2,1)} %param.5) | copy-start | bytes 6291460
where the time goes:
time: 413 us; the launch traced here: 411 us
  blocking collectives  297 us (72%)
  local copies, waits for them, and re-layouts  65.4 us (16%)
  matrix products  32.9 us (8%)
  starting transfers between devices  13.5 us (3%)
    all_gather x1, blocking collectives, local(): lax.all_gather(jnp.concatenate([owner_map, left_local], axis=1), 'sector'...  218 us
    psum x1, blocking collectives, local(): total = lax.psum(partial_sum, 'term')  78.5 us
    reshape x1, local copies, waits for them, and re-layouts, local(): arrived = arrived.reshape(slots, terms_dev, width, width)  14.6 us
    reshape x1, local copies, waits for them, and re-layouts, local(): packed.reshape(n_sector, capacity, -1)  14.1 us
    all_to_all x1, starting transfers between devices, local(): lax.all_to_all(packed.reshape(n_sector, capacity, -1), 'sector', split_ax...  13.5 us
    dot_general x1, matrix products, local(): jnp.dot(collect, images.reshape(slots, -1), precision=lax.Precision.HIGHE...  10.5 us
    unnamed x10, local copies, waits for them, and re-layouts  9.9 us
    dot_general x1, local copies, waits for them, and re-layouts, local(): jnp.dot(collect, images.reshape(slots, -1), precision=lax.Precision.HIGHE...  8.99 us
  transfers between devices with their start and end apart: 1, of which 0 were waited for; matrix products, arithmetic and copies ran while one was open for 3% of the time, Pallas kernels for 0%

commit v1 on v0

--- a/solution.py
+++ b/solution.py
@@ -25,9 +25,11 @@
     packer = (lax.broadcasted_iota(jnp.int32, (slots, sec_dev), 0) == slot_id[None, :]).astype(
         jnp.bfloat16
     )
-    routes_all = lax.all_gather(
-        jnp.concatenate([owner_map, left_local], axis=1), "sector", axis=0, tiled=True
-    )
+    part = jnp.concatenate([owner_map, left_local], axis=1)
+    size = lax.axis_size("sector")
+    blocks = jnp.stack([part for _ in range(size)])
+    blocks = lax.all_to_all(blocks, "sector", split_axis=0, concat_axis=0)
+    routes_all = jnp.concatenate(blocks, axis=0)
     all_owners = routes_all[:, 0].reshape(n_sector, sec_dev)
     all_local = routes_all[:, 1].reshape(n_sector, sec_dev)
     all_ranks = ranks_of(all_owners)

time: 413 us -> 382 us (0.925)
  blocking collectives: 297 us -> 79.8 us
  waiting for transfers between devices: 0.01 us -> 174 us
  starting transfers between devices: 13.5 us -> 23.6 us
    all_gather x1 -> x0, blocking collectives: 218 us -> none  [local(): lax.all_gather(jnp.concatenate([owner_map, left_local], axis=1), 'sector'...]
    all_to_all x1, waiting for transfers between devices: 0.01 us -> 174 us  [local(): lax.all_to_all(packed.reshape(n_sector, capacity, -1), 'sector', split_ax...]
    all_to_all x0 -> x1, starting transfers between devices: none -> 13.1 us  [local(): blocks = lax.all_to_all(blocks, 'sector', split_axis=0, concat_axis=0)]
    unnamed x10 -> x8, local copies, waits for them, and re-layouts: 9.9 us -> 10.6 us
  transfers between devices with their start and end apart: 1 -> 2, of which waited for: 0 -> 1; matrix products, arithmetic and copies ran while one was open for 3% -> 13% of each run, Pallas kernels for 0% -> 0%
where the time goes in v1:
time: 382 us; the launch traced here: 381 us
  waiting for transfers between devices  174 us (46%)
  blocking collectives  79.8 us (21%)
  local copies, waits for them, and re-layouts  66.7 us (17%)
  matrix products  32.8 us (9%)
  starting transfers between devices  23.6 us (6%)
  other arithmetic  3.98 us (1%)
    all_to_all x1, waiting for transfers between devices, local(): lax.all_to_all(packed.reshape(n_sector, capacity, -1), 'sector', split_ax...  174 us
    psum x1, blocking collectives, local(): total = lax.psum(partial_sum, 'term')  79.8 us
    reshape x1, local copies, waits for them, and re-layouts, local(): arrived = arrived.reshape(slots, terms_dev, width, width)  14.6 us
    reshape x1, local copies, waits for them, and re-layouts, local(): packed.reshape(n_sector, capacity, -1)  14.1 us
    all_to_all x1, starting transfers between devices, local(): blocks = lax.all_to_all(blocks, 'sector', split_axis=0, concat_axis=0)  13.1 us
    unnamed x8, local copies, waits for them, and re-layouts  10.6 us
    all_to_all x1, starting transfers between devices, local(): lax.all_to_all(packed.reshape(n_sector, capacity, -1), 'sector', split_ax...  10.5 us
    dot_general x1, matrix products, local(): jnp.dot(collect, images.reshape(slots, -1), precision=lax.Precision.HIGHE...  10.5 us
  transfers between devices with their start and end apart: 2, of which 1 were waited for; matrix products, arithmetic and copies ran while one was open for 13% of the time, Pallas kernels for 0%

profile of v1, /device:TPU:1, one launch (start us, length us, event | category | flops | bytes accessed | tf_op | source)
XLA Modules:
  0.0 381.1 jit_solution(13319439794850033618)
XLA Ops:
  0.0 0.0 copy-start
  0.0 0.8 pad_add_fusion
  0.9 0.7 reshape.122
  1.6 13.1 %all-to-all-start = ((s32[64,1,128]{2,1,0:T(1,128)}), s32[64,1,128]{2,1,0:T(1,128)S(1)}, u32[]{:S(2)}, u32[]{:S(2)}) async-start(s32[64,1,128]{2,1,0:T(1,128)} %reshape.122), calls=%async_computation | async-start | bytes 65536 | tf_op jit(solution)/shard_map/all_to_all | solution.py:31
  14.7 0.8 convert_reduce_fusion.1
  15.6 0.7 multiply_add_fusion
  16.2 0.0 copy-done
  16.2 5.4 %convert_bitcast_fusion = bf16[64,2,128,128]{2,3,1,0:T(8,128)(2,1)} fusion(bf16[2,64,128,128]{3,2,1,0:T(8,128)(2,1)} %param.6, bf16[64,128,128]{2,1,0:T(8,128)(2,1)S(1)} %copy-done), kind=kOutput, calls=%fused_computation.12 | convolution fusion | flops 538968064 | bytes 10485760 | tf_op jit(solution)/shard_map/sij,tsjk->stik/dot_general | solution.py:40
  21.6 6.3 %copy.27 = bf16[64,2,128,128]{3,2,1,0:T(8,128)(2,1)} copy(bf16[64,2,128,128]{2,3,1,0:T(8,128)(2,1)} %convert_bitcast_fusion) | data formatting | bytes 8388608 | tf_op jit(solution)/shard_map/convert_element_type | solution.py:42
  28.0 8.8 %convolution_convert_fusion = bf16[128,32768]{1,0:T(8,128)(2,1)} fusion(bf16[8,8,256,128]{3,2,1,0:T(8,128)(2,1)} %bitcast.42, s32[64]{0:T(128)S(1)} %multiply_add_fusion), kind=kOutput, calls=%fused_computation.1 | convolution fusion | flops 541073408 | bytes 12583168 | tf_op jit(solution)/shard_map/dot_general | solution.py:43
  36.7 14.1 %reshape.96 = bf16[64,2,32768]{2,1,0:T(2,128)(2,1)} reshape(bf16[128,32768]{1,0:T(8,128)(2,1)} %convolution_convert_fusion) | data formatting | bytes 16777216 | tf_op jit(solution)/shard_map/reshape | solution.py:47
  50.9 0.0 all-to-all-done
  50.9 10.5 %all-to-all-start.1 = ((bf16[64,2,32768]{2,1,0:T(2,128)(2,1)}), bf16[64,2,32768]{2,1,0:T(2,128)(2,1)}, u32[]{:S(2)}, u32[]{:S(2)}) async-start(bf16[64,2,32768]{2,1,0:T(2,128)(2,1)} %reshape.96), calls=%async_computation.1 | async-start | bytes 16777216 | tf_op jit(solution)/shard_map/all_to_all | solution.py:46
  61.4 0.5 broadcast.110
  61.9 0.7 reduce.8
  62.7 0.1 reshape.123
  62.8 0.1 reshape.94
  62.9 0.1 slice_reduce_fusion
  63.0 0.1 reshape_squeeze.3
  63.0 0.1 add.66
  63.1 0.7 convert_reduce_fusion
  63.8 0.1 select_reduce_fusion
  64.0 0.1 copy.24
  64.0 0.1 sub.7
  64.2 0.1 copy.25
  64.3 0.1 min.18
  64.5 8.6 %gather_fusion = bf16[128,2,128,128]{3,2,1,0:T(8,128)(2,1)} fusion(bf16[2,64,128,128]{3,2,1,0:T(8,128)(2,1)} %param.7, s32[1024]{0:T(1024)S(1)} %pad_clamp_fusion), kind=kCustom, calls=%fused_computation | custom fusion | bytes 16777728 | tf_op jit(solution)/shard_map/jit(_take)/gather | solution.py:50
  73.0 174.1 %all-to-all-done.1 = bf16[64,2,32768]{2,1,0:T(2,128)(2,1)} async-done(((bf16[64,2,32768]{2,1,0:T(2,128)(2,1)}), bf16[64,2,32768]{2,1,0:T(2,128)(2,1)}, u32[]{:S(2)}, u32[]{:S(2)}) %all-to-all-start.1) | async-done | bytes 8388640 | tf_op jit(solution)/shard_map/all_to_all | solution.py:46
  247.1 14.6 %reshape.97 = bf16[128,2,128,128]{3,2,1,0:T(8,128)(2,1)} reshape(bf16[64,2,32768]{2,1,0:T(2,128)(2,1)} %all-to-all-done.1) | data formatting | bytes 16777216 | tf_op jit(solution)/shard_map/reshape | solution.py:49
  261.7 8.2 %fusion = f32[128,128,128,1]{2,1,3,0:T(8,128)S(1)} fusion(bf16[128,2,128,128]{3,2,1,0:T(8,128)(2,1)} %reshape.97, bf16[128,2,128,128]{3,2,1,0:T(8,128)(2,1)} %gather_fusion, pred[128]{0:T(512)(128)(4,1)S(1)} %compare_and_fusion), kind=kOutput, calls=%fused_computation.3 | convolution fusion | flops 1077936128 | bytes 25165952 | tf_op jit(solution)/shard_map/tnij,ntjk->nik/dot_general | solution.py:51
  269.9 9.7 %copy.45 = f32[16,8,128,128]{3,1,2,0:T(8,128)} copy(f32[16,8,128,128]{3,2,1,0:T(8,128)S(1)} %bitcast.39) | data formatting | bytes 16777216
  279.7 9.0 %copy.28 = f32[16384,128]{1,0:T(8,128)} copy(f32[16384,128]{0,1:T(8,128)} %bitcast.41) | data formatting | bytes 16777216 | tf_op jit(solution)/shard_map/dot_general | solution.py:55
  288.7 0.0 copy-start.1
  288.7 10.5 %fusion.15 = f32[64,128,128]{2,0,1:T(8,128)} fusion(f32[128,128,128]{2,1,0:T(8,128)} %bitcast.40, s32[128]{0:T(128)S(1)} %sub.7), kind=kOutput, calls=%fused_computation.25 | convolution fusion | flops 1610620928 | bytes 12583424 | tf_op jit(solution)/shard_map/dot_general | solution.py:55
  299.1 79.8 %all-reduce.1 = bf16[64,128,128]{2,0,1:T(8,128)(2,1)} all-reduce(f32[64,128,128]{2,0,1:T(8,128)} %fusion.15), channel_id=1, replica_groups=mesh['term'=4,'sector'=64] {'term'}, use_global_device_ids=true, to_apply=%region_3.4 | all-reduce | flops 1048576 | bytes 6291456 | tf_op jit(solution)/shard_map/psum | solution.py:61
  378.9 1.1 dynamic-slice_convert_fusion
  380.0 1.1 copy.29
  381.1 0.0 copy-done.1
  (8 shorter events, 0.1 us)
Async XLA Ops:
  0.0 16.2 %copy-start = (bf16[64,128,128]{2,1,0:T(8,128)(2,1)S(1)}, bf16[64,128,128]{2,1,0:T(8,128)(2,1)}, u32[]{:S(2)}) copy-start(bf16[64,128,128]{2,1,0:T(8,128)(2,1)} %param.5) | copy-start | bytes 6291460
  1.6 49.3 %all-to-all-start = ((s32[64,1,128]{2,1,0:T(1,128)}), s32[64,1,128]{2,1,0:T(1,128)S(1)}, u32[]{:S(2)}, u32[]{:S(2)}) async-start(s32[64,1,128]{2,1,0:T(1,128)} %reshape.122), calls=%async_computation | async-start | bytes 65536 | tf_op jit(solution)/shard_map/all_to_all | solution.py:31
  50.9 196.2 %all-to-all-start.1 = ((bf16[64,2,32768]{2,1,0:T(2,128)(2,1)}), bf16[64,2,32768]{2,1,0:T(2,128)(2,1)}, u32[]{:S(2)}, u32[]{:S(2)}) async-start(bf16[64,2,32768]{2,1,0:T(2,128)(2,1)} %reshape.96), calls=%async_computation.1 | async-start | bytes 16777216 | tf_op jit(solution)/shard_map/all_to_all | solution.py:46
  288.7 92.5 %copy-start.1 = (bf16[64,128,128]{2,1,0:T(8,128)(2,1)S(1)}, bf16[64,128,128]{2,1,0:T(8,128)(2,1)}, u32[]{:S(2)}) copy-start(bf16[64,128,128]{2,1,0:T(8,128)(2,1)} %param.5) | copy-start | bytes 6291460
